TPU v7x, 512 devices: a whole 4x4x16 slice. The times are simulated.
512 devices in a mesh: dp: 16 (over x, y), expert: 32 (over z, core).
Axes of the slice: x: 4, y: 4, z: 16, core: 2. Of those that a mesh axis runs over, the one named last changes fastest.
Arguments:
- tokens: bfloat16 [8192, 1024], P(('dp', 'expert')), may hold values from -6 to 6
- upstream: bfloat16 [8192, 1024], P(('dp', 'expert')), may hold values from -6 to 6
- expert_ids: int32 [8192, 8], P(('dp', 'expert')), may hold values from 0 to 127, all different within a row; in each aligned block of 16 rows (0 to 15, 16 to 31, ...) at most 2 rows name the same one
- gates: float32 [8192, 8], P(('dp', 'expert')), may hold values from 0.05 to 1
- relocate: int32 [32, 4], replicated, may hold values from 0 to 1, as said below
- w_gate_up: bfloat16 [32, 16, 384, 1024], P('expert', 'dp'), may hold values from -0.1875 to 0.1875
- w_down: bfloat16 [32, 16, 192, 1024], P('expert', 'dp'), may hold values from -0.21875 to 0.21875
Outputs:
- grad_tokens: bfloat16 [8192, 1024], P(('dp', 'expert'))
- grad_gate_up: bfloat16 [32, 16, 384, 1024], P('expert', 'dp')
- grad_down: bfloat16 [32, 16, 192, 1024], P('expert', 'dp')
Inputs may be any that keep to these rules, and one draw needn't show every extreme that they name: `expert_ids`: each row names 8 different experts; the rows of one device name one expert at most 2 times, and some device reaches 2. `relocate`: the first and the second half of the rows are equal; both values occur.
All inputs are finite; a program needn't handle non-finite values.
Results may differ from a plain program's by a relative error of at most 0.0064.
Values may be sent and summed in bfloat16 or wider, within the bound.
A program may use at most 64 MiB of HBM per device.

v0:
```python
import jax
import jax.numpy as jnp
from jax import lax
from jax.sharding import PartitionSpec as P

SLICES = 4
CAP = 2
contract_last = (((1,), (1,)), ((), ()))
contract_first = (((0,), (0,)), ((), ()))


def silu_parts(values_in):
    sigmoid_of = jax.nn.sigmoid(values_in)
    return (values_in * sigmoid_of, sigmoid_of * (1.0 + values_in * (1.0 - sigmoid_of)))


def half_swap(block, count, parity):
    half = count // 2
    route = [(c, (c + half) % count) for c in range(count) if c % 2 == parity]
    return lax.ppermute(block, "expert", route)


def three_parts(gates):
    first = lax.reduce_precision(gates, 8, 7)
    rest = gates - first
    second = lax.reduce_precision(rest, 8, 7)
    third = rest - second
    return [part.astype(jnp.bfloat16) for part in (first, second, third)]


def block_rank(hits, tok_dev):
    grouped = hits.reshape(hits.shape[0], -1, tok_dev)
    earlier = jnp.arange(tok_dev)[:, None] > jnp.arange(tok_dev)[None, :]
    ranks = jnp.sum(jnp.where(earlier[None, None], grouped[:, :, None, :], 0), axis=-1)
    return ranks.reshape(hits.shape)


def per_device(tokens, upstream, expert_ids, gates, relocate, w_gate_up, w_down):
    n_rows = lax.axis_size("dp")
    n_cols = lax.axis_size("expert")
    slots = n_rows // SLICES
    experts = slots * n_cols
    tok_dev, width = tokens.shape
    top = expert_ids.shape[1]
    slice_width = w_down.shape[2]
    half = n_cols // 2
    col = lax.axis_index("expert")
    slot_here = lax.axis_index("dp") // SLICES
    y_groups = [[x * SLICES + y for y in range(SLICES)] for x in range(slots)]
    x_groups = [[x * SLICES + y for x in range(slots)] for y in range(SLICES)]
    own_pack = jnp.concatenate([w_gate_up[0, 0], w_down[0, 0]], axis=0)
    far_pack = half_swap(own_pack, n_cols, 0)
    meta = jnp.concatenate(
        [expert_ids.astype(jnp.bfloat16)]
        + three_parts(gates)
        + [jnp.zeros((tok_dev, 128 - 4 * top), jnp.bfloat16)],
        axis=1,
    )
    packed = jnp.concatenate([tokens, upstream, meta], axis=1)
    gathered = lax.all_gather(packed, "expert", axis=0, tiled=True)
    even = col % 2 == 0
    rel_row = jnp.sum(jnp.where(jnp.arange(n_cols)[:, None] == col, relocate, 0), axis=0)
    served = jnp.where(even, (col + half * rel_row) % n_cols, col) * slots + jnp.arange(slots)
    meta_all = gathered[:, 2 * width :].astype(jnp.float32)
    ids_all = meta_all[:, :top].astype(jnp.int32)
    gates_all = (
        meta_all[:, top : 2 * top] + meta_all[:, 2 * top : 3 * top] + meta_all[:, 3 * top : 4 * top]
    )
    match = ids_all[None] == served[:, None, None]
    hits = jnp.sum(match.astype(jnp.int32), axis=-1)
    gate_of = jnp.sum(jnp.where(match, gates_all[None], 0.0), axis=-1)
    n_tok = ids_all.shape[0]
    place = CAP * (jnp.arange(n_tok, dtype=jnp.int32) // tok_dev)[None] + block_rank(hits, tok_dev)
    seats = n_cols * CAP
    seat = (hits[:, None, :] > 0) & (
        place[:, None, :] == jnp.arange(seats, dtype=jnp.int32)[None, :, None]
    )
    select = seat.reshape(slots * seats, n_tok).astype(jnp.bfloat16)
    rows = jnp.dot(select, gathered[:, : 2 * width], preferred_element_type=jnp.float32)
    gate_rows = jnp.sum(jnp.where(seat, gate_of[:, None, :], 0.0), axis=-1).reshape(-1, 1)
    sent = jnp.concatenate(
        [rows[:, :width].astype(jnp.bfloat16), (gate_rows * rows[:, width:]).astype(jnp.bfloat16)],
        axis=1,
    )
    at_x = lax.all_to_all(
        sent, "dp", split_axis=0, concat_axis=0, axis_index_groups=x_groups, tiled=True
    )
    all_rows = lax.all_gather(at_x, "dp", axis=0, axis_index_groups=y_groups, tiled=True)
    rows_x = all_rows[:, :width]
    rows_d = all_rows[:, width:]
    rel_here = jnp.sum(jnp.where(jnp.arange(slots) == slot_here, rel_row, 0))
    pack = jnp.where(even & (rel_here == 1), far_pack, own_pack)
    gate_up = pack[: 2 * slice_width]
    down_rows = pack[2 * slice_width :]
    gate_and_up = lax.dot_general(
        rows_x, gate_up, contract_last, preferred_element_type=jnp.float32
    )
    gate_pre = gate_and_up[:, :slice_width]
    up_pre = gate_and_up[:, slice_width:]
    activated, slope_of = silu_parts(gate_pre)
    hidden = (activated * up_pre).astype(jnp.bfloat16)
    hidden_grad = lax.dot_general(
        rows_d, down_rows, contract_last, preferred_element_type=jnp.float32
    )
    pre_grads = jnp.concatenate(
        [
            (hidden_grad * up_pre * slope_of).astype(jnp.bfloat16),
            (hidden_grad * activated).astype(jnp.bfloat16),
        ],
        axis=1,
    )
    slice_part = jnp.dot(pre_grads, gate_up, preferred_element_type=jnp.float32).astype(
        jnp.bfloat16
    )
    grad_gu = lax.dot_general(
        pre_grads, rows_x, contract_first, preferred_element_type=jnp.float32
    ).astype(jnp.bfloat16)
    grad_dn = lax.dot_general(
        hidden, rows_d, contract_first, preferred_element_type=jnp.float32
    ).astype(jnp.bfloat16)
    grad_pack = jnp.concatenate([grad_gu, grad_dn], axis=0)
    far_grads = half_swap(grad_pack, n_cols, 1)
    grad_pack = jnp.where(~even & (rel_here == 1), far_grads, grad_pack)
    parts = lax.all_to_all(
        slice_part, "dp", split_axis=0, concat_axis=0, axis_index_groups=y_groups, tiled=True
    )
    summed = jnp.sum(
        parts.reshape(SLICES, slots * seats, width).astype(jnp.float32), axis=0
    ).astype(jnp.bfloat16)
    back = lax.all_to_all(
        summed, "dp", split_axis=0, concat_axis=0, axis_index_groups=x_groups, tiled=True
    )
    partial = lax.dot_general(select, back, contract_first, preferred_element_type=jnp.float32)
    grad_tokens = lax.psum_scatter(partial, "expert", scatter_dimension=0, tiled=True).astype(
        jnp.bfloat16
    )
    return (
        grad_tokens,
        grad_pack[: 2 * slice_width].reshape(w_gate_up.shape),
        grad_pack[2 * slice_width :].reshape(w_down.shape),
    )


def solution(mesh):
    return jax.shard_map(
        per_device,
        mesh=mesh,
        in_specs=(
            P(("dp", "expert"), None),
            P(("dp", "expert"), None),
            P(("dp", "expert"), None),
            P(("dp", "expert"), None),
            P(),
            P("expert", "dp", None, None),
            P("expert", "dp", None, None),
        ),
        out_specs=(
            P(("dp", "expert"), None),
            P("expert", "dp", None, None),
            P("expert", "dp", None, None),
        ),
        check_vma=False,
    )
```

profile of v0, /device:TPU:28, one launch (start us, length us, event | category | flops | bytes accessed | tf_op | source)
XLA Modules:
  0.0 352.9 jit_solution(1204173419493060899)
XLA Ops:
  7.2 0.8 copy.30
  8.0 0.8 copy.31
  8.7 1.5 concatenate.15
  10.4 0.8 select_reduce_fusion.2
  11.2 0.6 iota_add_fusion
  11.9 74.4 %all-gather.3.cloned.1.call-done = bf16[512,2176]{1,0:T(8,128)(2,1)} async-done(((bf16[16,2176]{1,0:T(8,128)(2,1)}), bf16[512,2176]{1,0:T(8,128)(2,1)}) %all-gather.3.cloned.1.call-update) | async-done | bytes 2228240 | tf_op jit(solution)/shard_map/all_gather | solution.py:60
  86.3 0.9 slice.65
  88.6 2.3 fusion
  91.2 17.6 %all_to_all.30 = bf16[4,64,2048]{2,1,0:T(8,128)(2,1)} all-to-all(bf16[4,64,2048]{2,1,0:T(8,128)(2,1)S(1)} %bitcast.21), channel_id=1, replica_groups={{0,128,256,384},{32,160,288,416},{64,192,320,448},{96,224,352,480},{1,1..., dimensions={0} | all-to-all | bytes 2097152 | tf_op jit(solution)/shard_map/all_to_all | solution.py:85
  109.0 8.5 %collective-permute-start = (bf16[576,1024]{1,0:T(8,128)(2,1)S(1)}, bf16[576,1024]{1,0:T(8,128)(2,1)S(1)}, u32[]{:S(2)}, u32[]{:S(2)}) collective-permute-start(bf16[576,1024]{1,0:T(8,128)(2,1)S(1)} %pad_maximum_fusion), channel_id=1, source_target_pairs={{0,16},{2,18},{4,20},{6,22},{8,24},{10,26},{12,28},{14,30},{16,0},... | collective-permute-start | bytes 3538952 | tf_op jit(solution)/shard_map/ppermute | solution.py:20
  118.2 44.6 %collective-permute-done = bf16[576,1024]{1,0:T(8,128)(2,1)S(1)} collective-permute-done((bf16[576,1024]{1,0:T(8,128)(2,1)S(1)}, bf16[576,1024]{1,0:T(8,128)(2,1)S(1)}, u32[]{:S(2)}, u32[]{:S(2)}) %collective-permute-start) | collective-permute-done | bytes 1179680 | tf_op jit(solution)/shard_map/ppermute | solution.py:20
  163.3 2.8 fusion.4
  166.1 1.0 multiply_convert_fusion.2
  167.3 1.3 convolution_convert_fusion
  168.6 26.8 %all_to_all.31 = bf16[4,256,1024]{2,1,0:T(8,128)(2,1)S(1)} all-to-all(bf16[4,256,1024]{2,1,0:T(8,128)(2,1)S(1)} %bitcast.24), channel_id=1, replica_groups={{0,32,64,96},{128,160,192,224},{256,288,320,352},{384,416,448,480},{1,3..., dimensions={0} | all-to-all | bytes 4194304 | tf_op jit(solution)/shard_map/all_to_all | solution.py:124
  195.8 10.0 %all_to_all.32 = bf16[4,64,1024]{2,1,0:T(8,128)(2,1)S(1)} all-to-all(bf16[4,64,1024]{2,1,0:T(8,128)(2,1)S(1)} %bitcast.25), channel_id=1, replica_groups={{0,128,256,384},{32,160,288,416},{64,192,320,448},{96,224,352,480},{1,1..., dimensions={0} | all-to-all | bytes 1048576 | tf_op jit(solution)/shard_map/all_to_all | solution.py:130
  205.7 1.8 convolution_bitcast_fusion
  207.6 2.7 fusion.10
  210.9 0.6 fusion.13
  211.6 0.7 collective-permute-start.1
  212.9 0.8 slice_bitcast_fusion.1
  213.6 0.9 slice_bitcast_fusion
  214.6 130.4 %reduce-scatter.2.cloned.1.call-done = f32[16,1024]{1,0:T(8,128)} async-done(((f32[512,1024]{1,0:T(8,128)}), f32[16,1024]{1,0:T(8,128)}) %reduce-scatter.2.cloned.1.call-update) | async-done | bytes 65552 | tf_op jit(solution)/shard_map/reduce_scatter | solution.py:134
  344.9 1.5 convert_element_type.60
  (51 shorter events, 4.2 us)
Async XLA Ops:
  7.2 79.2 %all-gather.3.cloned.1.call-start = ((), (), s32[]{:S(2)}) async-start(), calls=%async_computation.4 | async-start | bytes 2297856 | tf_op jit(solution)/shard_map/all_gather | solution.py:60
  10.3 153.0 %all-gather.5.cloned.1.call-start = ((), (), s32[]{:S(2)}) async-start(), calls=%async_computation.5 | async-start | bytes 5242880 | tf_op jit(solution)/shard_map/all_gather | solution.py:88
  91.2 17.7 %copy-start = (bf16[1,1,384,1024]{3,2,1,0:T(8,128)(2,1)S(1)}, bf16[1,1,384,1024]{3,2,1,0:T(8,128)(2,1)}, u32[]{:S(2)}) copy-start(bf16[1,1,384,1024]{3,2,1,0:T(8,128)(2,1)} %param.12) | copy-start | bytes 2359300
  91.2 17.7 %copy-start.1 = (bf16[1,1,192,1024]{3,2,1,0:T(8,128)(2,1)S(1)}, bf16[1,1,192,1024]{3,2,1,0:T(8,128)(2,1)}, u32[]{:S(2)}) copy-start(bf16[1,1,192,1024]{3,2,1,0:T(8,128)(2,1)} %param.13) | copy-start | bytes 1179652
  108.9 236.1 %reduce-scatter.2.cloned.1.call-start = ((), (), s32[]{:S(2)}) async-start(), calls=%async_computation.6 | async-start | bytes 2162688 | tf_op jit(solution)/shard_map/reduce_scatter | solution.py:134
  109.0 53.8 %collective-permute-start = (bf16[576,1024]{1,0:T(8,128)(2,1)S(1)}, bf16[576,1024]{1,0:T(8,128)(2,1)S(1)}, u32[]{:S(2)}, u32[]{:S(2)}) collective-permute-start(bf16[576,1024]{1,0:T(8,128)(2,1)S(1)} %pad_maximum_fusion), channel_id=1, source_target_pairs={{0,16},{2,18},{4,20},{6,22},{8,24},{10,26},{12,28},{14,30},{16,0},... | collective-permute-start | bytes 3538952 | tf_op jit(solution)/shard_map/ppermute | solution.py:20
  163.3 2.8 copy-start.2
  166.1 1.1 copy-start.4
  207.6 2.8 copy-start.3
  207.6 3.3 copy-start.5
  211.6 0.8 collective-permute-start.1
Sparse Core Ops, SparseCore 0:
  10.7 75.6 all-gather.2
  109.0 51.6 all-gather.4
  207.7 137.2 reduce-scatter.1
where the time goes:
time: 353 us
  waiting for transfers between devices  249 us (71%)
  blocking collectives  54.3 us (15%)
  between operations  14.7 us (4%)
  matrix products  12.6 us (4%)
  starting transfers between devices  9.4 us (3%)
  local copies, waits for them, and re-layouts  7.02 us (2%)
  other arithmetic  5.47 us (2%)
    reduce_scatter x1, waiting for transfers between devices, per_device(): lax.psum_scatter(partial, 'expert', scatter_dimension=0, tiled=True)  130 us
    all_gather x1, waiting for transfers between devices, per_device(): gathered = lax.all_gather(packed, 'expert', axis=0, tiled=True)  74.4 us
    ppermute x2, waiting for transfers between devices, half_swap(): return lax.ppermute(block, 'expert', route)  44.6 us
    all_to_all x1, blocking collectives, per_device(): lax.all_to_all(slice_part, 'dp', split_axis=0, concat_axis=0, axis_index_...  26.8 us
    all_to_all x1, blocking collectives, per_device(): lax.all_to_all(sent, 'dp', split_axis=0, concat_axis=0, axis_index_groups...  17.6 us
    all_to_all x1, blocking collectives, per_device(): lax.all_to_all(summed, 'dp', split_axis=0, concat_axis=0, axis_index_grou...  9.97 us
    ppermute x2, starting transfers between devices, half_swap(): return lax.ppermute(block, 'expert', route)  9.28 us
  transfers between devices with their start and end apart: 5, of which 3 were waited for; matrix products, arithmetic and copies ran while one was open for 2% of the time, Pallas kernels for 0%

commit v1 on v0

--- a/solution.py
+++ b/solution.py
@@ -57,7 +57,8 @@
         axis=1,
     )
     packed = jnp.concatenate([tokens, upstream, meta], axis=1)
-    gathered = lax.all_gather(packed, "expert", axis=0, tiled=True)
+    outgoing = jnp.stack([packed] * lax.axis_size("expert"))
+    gathered = jnp.concatenate(lax.all_to_all(outgoing, "expert", 0, 0), axis=0)
     even = col % 2 == 0
     rel_row = jnp.sum(jnp.where(jnp.arange(n_cols)[:, None] == col, relocate, 0), axis=0)
     served = jnp.where(even, (col + half * rel_row) % n_cols, col) * slots + jnp.arange(slots)

time: 353 us -> 400 us (1.13)
  the two profiles are of different devices: /device:TPU:28 before, /device:TPU:2 now
where the time goes in v1:
time: 400 us; the launch traced here: 399 us
  waiting for transfers between devices  291 us (73%)
  blocking collectives  50.6 us (13%)
  starting transfers between devices  19.6 us (5%)
  between operations  15 us (4%)
  matrix products  11 us (3%)
  other arithmetic  6.12 us (2%)
  local copies, waits for them, and re-layouts  5.86 us (1%)
    reduce_scatter x1, waiting for transfers between devices, per_device(): lax.psum_scatter(partial, 'expert', scatter_dimension=0, tiled=True)  135 us
    all_to_all x1, waiting for transfers between devices, per_device(): gathered = jnp.concatenate(lax.all_to_all(outgoing, 'expert', 0, 0), axis=0)  103 us
    ppermute x2, waiting for transfers between devices, half_swap(): return lax.ppermute(block, 'expert', route)  53.1 us
    all_to_all x1, blocking collectives, per_device(): lax.all_to_all(slice_part, 'dp', split_axis=0, concat_axis=0, axis_index_...  21.2 us
    all_to_all x1, blocking collectives, per_device(): lax.all_to_all(sent, 'dp', split_axis=0, concat_axis=0, axis_index_groups...  18.2 us
    all_to_all x1, starting transfers between devices, per_device(): gathered = jnp.concatenate(lax.all_to_all(outgoing, 'expert', 0, 0), axis=0)  15.6 us
    all_to_all x1, blocking collectives, per_device(): lax.all_to_all(summed, 'dp', split_axis=0, concat_axis=0, axis_index_grou...  11.2 us
  transfers between devices with their start and end apart: 5, of which 3 were waited for; matrix products, arithmetic and copies ran while one was open for 2% of the time, Pallas kernels for 0%

profile of v1, /device:TPU:2, one launch (start us, length us, event | category | flops | bytes accessed | tf_op | source)
XLA Modules:
  0.0 399.5 jit_solution(15823126766946920039)
XLA Ops:
  7.2 0.7 convert_element_type.49
  7.9 0.7 fusion.29
  8.9 0.9 concatenate.15
  9.8 1.5 stack.2
  11.3 15.6 %all-to-all-start = ((bf16[32,16,2176]{2,1,0:T(8,128)(2,1)}), bf16[32,16,2176]{2,1,0:T(8,128)(2,1)S(1)}, u32[]{:S(2)}, u32[]{:S(2)}) async-start(bf16[32,16,2176]{2,1,0:T(8,128)(2,1)} %stack.2), calls=%async_computation | async-start | bytes 4456448 | tf_op jit(solution)/shard_map/all_to_all | solution.py:61
  27.2 0.6 iota_add_fusion
  27.9 103.4 %all-to-all-done = bf16[32,16,2176]{2,1,0:T(8,128)(2,1)S(1)} async-done(((bf16[32,16,2176]{2,1,0:T(8,128)(2,1)}), bf16[32,16,2176]{2,1,0:T(8,128)(2,1)S(1)}, u32[]{:S(2)}, u32[]{:S(2)}) %all-to-all-start) | async-done | bytes 2228256 | tf_op jit(solution)/shard_map/all_to_all | solution.py:61
  132.6 0.7 fusion
  133.6 18.2 %all_to_all.35 = bf16[4,64,2048]{2,1,0:T(8,128)(2,1)} all-to-all(bf16[4,64,2048]{2,1,0:T(8,128)(2,1)S(1)} %bitcast.24), channel_id=1, replica_groups={{0,128,256,384},{32,160,288,416},{64,192,320,448},{96,224,352,480},{1,1..., dimensions={0} | all-to-all | bytes 2097152 | tf_op jit(solution)/shard_map/all_to_all | solution.py:86
  152.0 3.2 collective-permute-start
  155.9 53.1 %collective-permute-done = bf16[576,1024]{1,0:T(8,128)(2,1)S(1)} collective-permute-done((bf16[576,1024]{1,0:T(8,128)(2,1)S(1)}, bf16[576,1024]{1,0:T(8,128)(2,1)S(1)}, u32[]{:S(2)}, u32[]{:S(2)}) %collective-permute-start) | collective-permute-done | bytes 1179680 | tf_op jit(solution)/shard_map/ppermute | solution.py:20
  209.4 2.7 fusion.4
  212.3 1.1 multiply_convert_fusion.2
  213.4 1.3 convolution_convert_fusion
  214.7 21.2 %all_to_all.36 = bf16[4,256,1024]{2,1,0:T(8,128)(2,1)S(1)} all-to-all(bf16[4,256,1024]{2,1,0:T(8,128)(2,1)S(1)} %bitcast.27), channel_id=1, replica_groups={{0,32,64,96},{128,160,192,224},{256,288,320,352},{384,416,448,480},{1,3..., dimensions={0} | all-to-all | bytes 4194304 | tf_op jit(solution)/shard_map/all_to_all | solution.py:125
  236.3 11.2 %all_to_all.37 = bf16[4,64,1024]{2,1,0:T(8,128)(2,1)S(1)} all-to-all(bf16[4,64,1024]{2,1,0:T(8,128)(2,1)S(1)} %bitcast.28), channel_id=1, replica_groups={{0,128,256,384},{32,160,288,416},{64,192,320,448},{96,224,352,480},{1,1..., dimensions={0} | all-to-all | bytes 1048576 | tf_op jit(solution)/shard_map/all_to_all | solution.py:131
  247.6 1.8 convolution_bitcast_fusion
  249.4 2.7 fusion.10
  252.7 0.6 fusion.13
  253.4 0.7 collective-permute-start.1
  254.7 0.8 slice_bitcast_fusion.1
  255.5 0.9 slice_bitcast_fusion
  256.4 134.8 %reduce-scatter.2.cloned.1.call-done = f32[16,1024]{1,0:T(8,128)} async-done(((f32[512,1024]{1,0:T(8,128)}), f32[16,1024]{1,0:T(8,128)}) %reduce-scatter.2.cloned.1.call-update) | async-done | bytes 65552 | tf_op jit(solution)/shard_map/reduce_scatter | solution.py:135
  391.2 1.5 convert_element_type.60
  (55 shorter events, 4.5 us)
Async XLA Ops:
  11.3 15.8 %copy-start.2 = (s32[32,4]{0,1:T(4,128)S(1)}, s32[32,4]{0,1:T(4,128)}, u32[]{:S(2)}) copy-start(s32[32,4]{0,1:T(4,128)} %param.11) | copy-start | bytes 1540
  11.3 119.9 %all-to-all-start = ((bf16[32,16,2176]{2,1,0:T(8,128)(2,1)}), bf16[32,16,2176]{2,1,0:T(8,128)(2,1)S(1)}, u32[]{:S(2)}, u32[]{:S(2)}) async-start(bf16[32,16,2176]{2,1,0:T(8,128)(2,1)} %stack.2), calls=%async_computation | async-start | bytes 4456448 | tf_op jit(solution)/shard_map/all_to_all | solution.py:61
  26.9 182.5 %all-gather.2.cloned.1.call-start = ((), (), s32[]{:S(2)}) async-start(), calls=%async_computation.5 | async-start | bytes 5242880 | tf_op jit(solution)/shard_map/all_gather | solution.py:89
  133.6 18.3 %copy-start = (bf16[1,1,384,1024]{3,2,1,0:T(8,128)(2,1)S(1)}, bf16[1,1,384,1024]{3,2,1,0:T(8,128)(2,1)}, u32[]{:S(2)}) copy-start(bf16[1,1,384,1024]{3,2,1,0:T(8,128)(2,1)} %param.12) | copy-start | bytes 2359300
  133.6 18.3 %copy-start.1 = (bf16[1,1,192,1024]{3,2,1,0:T(8,128)(2,1)S(1)}, bf16[1,1,192,1024]{3,2,1,0:T(8,128)(2,1)}, u32[]{:S(2)}) copy-start(bf16[1,1,192,1024]{3,2,1,0:T(8,128)(2,1)} %param.13) | copy-start | bytes 1179652
  151.9 239.3 %reduce-scatter.2.cloned.1.call-start = ((), (), s32[]{:S(2)}) async-start(), calls=%async_computation.6 | async-start | bytes 2162688 | tf_op jit(solution)/shard_map/reduce_scatter | solution.py:135
  152.0 56.9 %collective-permute-start = (bf16[576,1024]{1,0:T(8,128)(2,1)S(1)}, bf16[576,1024]{1,0:T(8,128)(2,1)S(1)}, u32[]{:S(2)}, u32[]{:S(2)}) collective-permute-start(bf16[576,1024]{1,0:T(8,128)(2,1)S(1)} %pad_maximum_fusion), channel_id=1, source_target_pairs={{0,16},{2,18},{4,20},{6,22},{8,24},{10,26},{12,28},{14,30},{16,0},... | collective-permute-start | bytes 3538952 | tf_op jit(solution)/shard_map/ppermute | solution.py:20
  209.4 2.8 copy-start.3
  212.3 1.1 copy-start.5
  249.4 2.8 copy-start.4
  249.4 3.3 copy-start.6
  253.4 0.8 collective-permute-start.1
Sparse Core Ops, SparseCore 0:
  152.0 49.2 all-gather.1
  249.5 141.6 reduce-scatter.1
